TPU v7x, 512 devices: a whole 4x8x8 slice. The times are simulated.
512 devices in a mesh: rep: 8 (over z_hi, core), dp: 64 (over z_lo, x, y).
Axes of the slice: x: 4, y: 8, z: 8 (z_hi: 4, z_lo: 2; z = z_hi * 2 + z_lo), core: 2. Of those that a mesh axis runs over, the one named last changes fastest.
Arguments:
- frames: bfloat16 [98304, 1536], P(('rep', 'dp')), may hold values from -6 to 6
- lengths: int32 [512, 8], P(('rep', 'dp')), may hold values from 0 to 192, as said below
- destination: int32 [512, 48], P(('rep', 'dp')), may hold values from -1 to 63, as said below
- kernel: float32 [15, 1536], replicated, may hold values from -1.5 to 1.5
- norm_gain: float32 [1536], replicated, may hold values from 0.5 to 1.5
- master: float32 [1536, 1536], P('dp'), may hold values from -0.15625 to 0.15625
- moment: float32 [1536, 1536], P('dp'), may hold values from -0.18 to 0.18
- second: float32 [1536, 1536], P('dp'), may hold values from 0.0003 to 0.003
- gradient: float32 [1536, 1536], P('dp'), may hold values from -1.8 to 1.8
- bucket_order: int32 [64], replicated, may hold values from 0 to 63, each once
- cotangent: bfloat16 [65536, 1536], P(('rep', 'dp')), may hold values from -6 to 6
Outputs:
- projected: bfloat16 [65536, 1536], P(('rep', 'dp'))
- frame_grad: bfloat16 [98304, 1536], P(('rep', 'dp'))
- kernel_grad: float32 [15, 1536], replicated
- gain_grad: float32 [1536], replicated
- new_master: float32 [1536, 1536], P('dp')
Inputs may be any that keep to these rules, and one draw needn't show every extreme that they name: destination[i, b] is the device of i's replica group that takes block b of device i, or -1 for a block without frames; a device's blocks with frames come first and go to distinct devices; every device receives exactly 32 blocks. A device's lengths add up to 4 times the number of its blocks that destination sends.
All inputs are finite; a program needn't handle non-finite values.
Results may differ from a plain program's by a relative error of at most 0.012.
Values may be sent and summed in bfloat16 or wider, within the bound.
No kernel may reach another device: no remote copies, remote signals or barrier semaphores. Data moves between devices by JAX's collectives and lax.ppermute only.
A program may use at most 128 MiB of HBM per device.

v0:
```python
import math
import jax
import jax.numpy as jnp
from jax import lax
from jax.sharding import PartitionSpec as P

ROWS = 128


def adam_step(master, moment, second, gradient):
    moment_new = 0.9 * moment + 0.1 * gradient
    second_new = 0.999 * second + 0.001 * jnp.square(gradient)
    return master - 0.01 * (moment_new / (jnp.sqrt(second_new) + 1e-08) + 0.1 * master)


def layout(lengths_row, height):
    bounds = jnp.cumsum(lengths_row)
    position = jnp.arange(height, dtype=jnp.int32)
    segment = jnp.sum((position[:, None] >= bounds[None, :]).astype(jnp.int32), axis=1)
    living = (position < bounds[-1]).astype(jnp.float32)
    return (segment, living)


def activate(frames_f, kernel, norm_gain, segment, living):
    height = frames_f.shape[0]
    half_width = (kernel.shape[0] - 1) // 2
    padded = jnp.pad(frames_f, ((half_width, half_width), (0, 0)))
    padded_seg = jnp.pad(segment, (half_width, half_width), constant_values=-1)
    mixed_sum = jnp.zeros_like(frames_f)
    for tap_index in range(kernel.shape[0]):
        inside = (lax.slice_in_dim(padded_seg, tap_index, tap_index + height) == segment).astype(
            frames_f.dtype
        )
        mixed_sum = (
            mixed_sum
            + kernel[tap_index]
            * lax.slice_in_dim(padded, tap_index, tap_index + height)
            * inside[:, None]
        )
    mixed_sum = mixed_sum * living[:, None]
    center = jnp.mean(mixed_sum, axis=1, keepdims=True)
    spread = jnp.mean(jnp.square(mixed_sum - center), axis=1, keepdims=True)
    scaled = (mixed_sum - center) * lax.rsqrt(spread + 1e-05) * norm_gain
    return scaled * jax.nn.sigmoid(scaled)


def to_owners(payload, sending, has_block, blocks, block_rows, received_blocks):
    columns = payload.shape[1]
    outgoing = jnp.einsum(
        "pn,nf->pf",
        sending,
        payload.reshape(blocks, block_rows * columns),
        preferred_element_type=jnp.float32,
    ).astype(jnp.bfloat16)
    incoming, arrived = (
        lax.all_to_all(outgoing, "dp", split_axis=0, concat_axis=0, tiled=True),
        lax.all_to_all(has_block, "dp", split_axis=0, concat_axis=0, tiled=True),
    )
    arrived_flag = arrived[:, 0].astype(jnp.float32)
    ranking = jnp.cumsum(arrived_flag) - 1.0
    wanted = jnp.arange(received_blocks).astype(jnp.float32)
    picking = ((ranking[None, :] == wanted[:, None]) & (arrived_flag[None, :] > 0.5)).astype(
        jnp.bfloat16
    )
    compact = jnp.einsum("mp,pf->mf", picking, incoming, preferred_element_type=jnp.float32).astype(
        jnp.bfloat16
    )
    return (compact.reshape(received_blocks * block_rows, columns), picking)


def to_sources(payload, picking, sending, blocks, block_rows, received_blocks):
    columns = payload.shape[1]
    outgoing = jnp.einsum(
        "mp,mf->pf",
        picking,
        payload.reshape(received_blocks, block_rows * columns),
        preferred_element_type=jnp.float32,
    ).astype(jnp.bfloat16)
    incoming = lax.all_to_all(outgoing, "dp", split_axis=0, concat_axis=0, tiled=True)
    homed = jnp.einsum("pn,pf->nf", sending, incoming, preferred_element_type=jnp.float32).astype(
        jnp.bfloat16
    )
    return homed.reshape(blocks * block_rows, columns)


def body(
    frames,
    lengths,
    destination,
    kernel,
    norm_gain,
    master,
    moment,
    second,
    gradient,
    bucket_order,
    cotangent,
):
    owners = lax.axis_size("dp")
    columns = frames.shape[1]
    updated = adam_step(master, moment, second, gradient)
    bucket = updated.astype(jnp.bfloat16)
    bucket_rows = bucket.shape[0]
    gathered = lax.all_gather(bucket, "dp", axis=0, tiled=True)
    weight = jnp.take(gathered.reshape(owners, bucket_rows, columns), bucket_order, axis=0).reshape(
        owners * bucket_rows, columns
    )
    height = frames.shape[0]
    blocks = destination.shape[1]
    block_rows = height // blocks
    received_blocks = cotangent.shape[0] // block_rows
    segment, living = layout(lengths[0], height)
    activated, pullback = jax.vjp(
        lambda inputs, kernel_in, gain_in: activate(inputs, kernel_in, gain_in, segment, living),
        frames.astype(jnp.float32),
        kernel,
        norm_gain,
    )
    moved_rows = activated.astype(jnp.bfloat16)
    targets = jnp.arange(owners, dtype=jnp.int32)
    sending = (destination[0][None, :] == targets[:, None]).astype(jnp.bfloat16)
    has_block = jnp.sum(sending, axis=1, keepdims=True)
    dims_back = (((1,), (1,)), ((), ()))
    source_proj = jnp.dot(moved_rows, weight, preferred_element_type=jnp.float32).astype(
        jnp.bfloat16
    )
    projected, picking = to_owners(
        source_proj, sending, has_block, blocks, block_rows, received_blocks
    )
    cot_home = to_sources(cotangent, picking, sending, blocks, block_rows, received_blocks)
    returned = lax.dot_general(
        cot_home, weight, dims_back, preferred_element_type=jnp.float32
    ).astype(jnp.bfloat16)
    frame_term, kernel_term, gain_term = pullback(returned.astype(jnp.float32))
    kernel_total, gain_total = lax.psum((kernel_term, gain_term), ("rep", "dp"))
    divisor = math.sqrt(lax.axis_size("rep") * owners * ROWS)
    return (
        projected,
        frame_term.astype(jnp.bfloat16),
        kernel_total / divisor,
        gain_total / divisor,
        updated,
    )


def solution(mesh):
    return jax.shard_map(
        body,
        mesh=mesh,
        in_specs=(
            P(("rep", "dp"), None),
            P(("rep", "dp"), None),
            P(("rep", "dp"), None),
            P(),
            P(),
            P("dp", None),
            P("dp", None),
            P("dp", None),
            P("dp", None),
            P(),
            P(("rep", "dp"), None),
        ),
        out_specs=(P(("rep", "dp"), None), P(("rep", "dp"), None), P(), P(), P("dp", None)),
        check_vma=False,
    )
```

profile of v0, /device:TPU:1, one launch (start us, length us, event | category | flops | bytes accessed | tf_op | source)
XLA Modules:
  0.0 658.0 jit_solution(7766027091813819460)
XLA Ops:
  7.2 2.0 fusion.27
  9.3 0.7 fusion.15
  10.0 0.7 copy.26
  10.7 12.9 %all-to-all-start = ((bf16[64,1,1]{2,1,0:T(2,128)(2,1)}), bf16[64,1,1]{2,1,0:T(2,128)(2,1)S(1)}, u32[]{:S(2)}, u32[]{:S(2)}) async-start(bf16[64,1,1]{2,1,0:T(2,128)(2,1)} %copy.26), calls=%async_computation | async-start | bytes 65536 | tf_op jit(solution)/shard_map/all_to_all | solution.py:57
  23.7 0.8 reduce-window.14
  24.5 0.6 slice.180
  25.1 0.7 compare_select_fusion
  25.8 0.6 pad_clamp_fusion
  26.4 0.7 compare_and_fusion.3
  27.1 1.3 compare_convert_fusion.13
  28.5 0.7 broadcast_in_dim.23
  29.6 3.3 all-to-all-done
  33.2 1.2 compare_reduce_fusion
  34.4 0.6 copy-done.86
  35.0 0.5 fusion
  35.5 0.5 broadcast.217
  36.0 1.1 reduce.36
  37.1 1.4 reshape.312
  38.6 7.8 %all-to-all-start.2 = ((bf16[64,2,3072]{2,1,0:T(2,128)(2,1)}), bf16[64,2,3072]{2,1,0:T(2,128)(2,1)S(1)}, u32[]{:S(2)}, u32[]{:S(2)}) async-start(bf16[64,2,3072]{2,1,0:T(2,128)(2,1)} %reshape.312), calls=%async_computation.2 | async-start | bytes 1572864 | tf_op jit(solution)/shard_map/all_to_all | solution.py:79
  47.0 3.9 fusion.26
  51.4 0.6 fusion.24
  52.0 19.9 %all-to-all-done.2 = bf16[64,2,3072]{2,1,0:T(2,128)(2,1)S(1)} async-done(((bf16[64,2,3072]{2,1,0:T(2,128)(2,1)}), bf16[64,2,3072]{2,1,0:T(2,128)(2,1)S(1)}, u32[]{:S(2)}, u32[]{:S(2)}) %all-to-all-start.2) | async-done | bytes 786464 | tf_op jit(solution)/shard_map/all_to_all | solution.py:79
  71.9 2.0 reshape.313
  73.8 2.1 convolution_convert_fusion.2
  75.9 1.2 reshape.267
  77.1 206.7 %all-gather.2.cloned.1.call-done = bf16[1536,1536]{1,0:T(8,128)(2,1)} async-done(((bf16[24,1536]{1,0:T(8,128)(2,1)}), bf16[1536,1536]{1,0:T(8,128)(2,1)}) %all-gather.2.cloned.1.call-update) | async-done | bytes 4718608 | tf_op jit(solution)/shard_map/all_gather | solution.py:104
  283.8 5.4 gather_fusion
  289.3 2.9 broadcast_select_fusion
  292.2 2.6 multiply_reduce_fusion
  294.9 0.3 multiply_reduce_fusion.18
  295.2 0.3 copy-done.49
  295.7 3.6 multiply_reduce_fusion.15
  299.4 4.3 multiply_reduce_fusion.5
  303.8 4.6 multiply_multiply_fusion.13
  308.4 0.9 bitcast_select_fusion
  309.3 2.0 convolution_convert_fusion.5
  311.4 2.3 reshape.264
  313.7 0.6 reshape.268
  314.3 0.6 reshape.269
  314.9 0.6 reshape.270
  315.5 0.6 reshape.271
  316.1 0.6 reshape.272
  316.7 0.6 reshape.273
  317.3 0.6 reshape.274
  317.9 0.6 reshape.276
  318.5 0.6 reshape.277
  319.1 1.5 fusion.1
  320.7 1.8 reduce.35
  322.5 3.2 reshape.310
  325.7 7.3 %all-to-all-start.1 = ((bf16[64,2,3072]{2,1,0:T(2,128)(2,1)}), bf16[64,2,3072]{2,1,0:T(2,128)(2,1)}, u32[]{:S(2)}, u32[]{:S(2)}) async-start(bf16[64,2,3072]{2,1,0:T(2,128)(2,1)} %reshape.310), calls=%async_computation.1 | async-start | bytes 1572864 | tf_op jit(solution)/shard_map/all_to_all | solution.py:56
  333.1 0.7 reshape.278
  333.8 0.7 reshape.279
  334.5 0.7 reshape.280
  335.2 0.7 reshape.281
  335.9 1.6 pad_add_fusion.6
  337.5 142.7 %psum.15 = f32[1536]{0:T(1024)S(1)} all-reduce(f32[1536]{0:T(1024)} %get-tuple-element.5), channel_id=1, replica_groups=mesh['rep'=8,'dp'=64] {'rep','dp'}, use_global_device_ids=true, to_apply=%region_26.27 | all-reduce | flops 1536 | bytes 12288 | tf_op jit(solution)/shard_map/psum | solution.py:135
  480.3 5.0 pad_add_fusion
  485.4 1.7 fusion.5
  487.0 0.6 broadcast_multiply_fusion.2
  487.6 155.4 %all-reduce.34.cloned.1.call-done = f32[15,1536]{1,0:T(8,128)} async-done(((f32[15,1536]{1,0:T(8,128)}), f32[15,1536]{1,0:T(8,128)}) %all-reduce.34.cloned.1.call-update) | async-done | bytes 92176 | tf_op jit(solution)/shard_map/psum | solution.py:135
  643.1 1.5 broadcast_multiply_fusion.1
  644.6 4.9 reshape.311
  649.6 0.6 convolution_convert_fusion.3
  650.2 1.0 reshape.265
  (214 shorter events, 2.0 us)
Async XLA Ops:
  7.2 22.0 %copy-start.9 = (bf16[128,1536]{1,0:T(8,128)(2,1)S(1)}, bf16[128,1536]{1,0:T(8,128)(2,1)}, u32[]{:S(2)}) copy-start(bf16[128,1536]{1,0:T(8,128)(2,1)} %param.21) | copy-start | bytes 1179652
  7.2 22.3 %copy-start.6 = (bf16[192,1536]{1,0:T(8,128)(2,1)S(1)}, bf16[192,1536]{1,0:T(8,128)(2,1)}, u32[]{:S(2)}) copy-start(bf16[192,1536]{1,0:T(8,128)(2,1)} %param.11) | copy-start | bytes 1769476
  7.2 276.6 %all-gather.2.cloned.1.call-start = ((), (), s32[]{:S(2)}) async-start(), calls=%async_computation.3 | async-start | bytes 4792320 | tf_op jit(solution)/shard_map/all_gather | solution.py:104
  10.7 22.2 %all-to-all-start = ((bf16[64,1,1]{2,1,0:T(2,128)(2,1)}), bf16[64,1,1]{2,1,0:T(2,128)(2,1)S(1)}, u32[]{:S(2)}, u32[]{:S(2)}) async-start(bf16[64,1,1]{2,1,0:T(2,128)(2,1)} %copy.26), calls=%async_computation | async-start | bytes 65536 | tf_op jit(solution)/shard_map/all_to_all | solution.py:57
  25.1 9.3 %copy-start.91 = (f32[32]{0:T(128)}, f32[32]{0:T(128)S(1)}, u32[]{:S(2)}) copy-start(f32[32]{0:T(128)S(1)} %iota_convert_fusion) | copy-start | bytes 388
  38.5 7.9 %copy-start.10 = (f32[15,1536]{1,0:T(8,128)S(1)}, f32[15,1536]{1,0:T(8,128)}, u32[]{:S(2)}) copy-start(f32[15,1536]{1,0:T(8,128)} %param.14) | copy-start | bytes 276484
  38.5 8.4 %copy-start.48 = (f32[192]{0:T(256)S(1)}, f32[192]{0:T(256)}, u32[]{:S(2)}) copy-start(f32[192]{0:T(256)} %get-tuple-element.71) | copy-start | bytes 2308
  38.5 8.4 %copy-start.68 = (f32[192]{0:T(256)S(1)}, f32[192]{0:T(256)}, u32[]{:S(2)}) copy-start(f32[192]{0:T(256)} %get-tuple-element.67) | copy-start | bytes 2308
  38.5 8.4 %copy-start.70 = (f32[192]{0:T(256)S(1)}, f32[192]{0:T(256)}, u32[]{:S(2)}) copy-start(f32[192]{0:T(256)} %get-tuple-element.68) | copy-start | bytes 2308
  38.5 8.5 %copy-start.72 = (f32[192]{0:T(256)S(1)}, f32[192]{0:T(256)}, u32[]{:S(2)}) copy-start(f32[192]{0:T(256)} %get-tuple-element.69) | copy-start | bytes 2308
  38.6 8.5 %copy-start.74 = (f32[192]{0:T(256)S(1)}, f32[192]{0:T(256)}, u32[]{:S(2)}) copy-start(f32[192]{0:T(256)} %get-tuple-element.70) | copy-start | bytes 2308
  38.6 8.5 %copy-start.76 = (f32[192]{0:T(256)S(1)}, f32[192]{0:T(256)}, u32[]{:S(2)}) copy-start(f32[192]{0:T(256)} %get-tuple-element.73) | copy-start | bytes 2308
  38.6 33.3 %all-to-all-start.2 = ((bf16[64,2,3072]{2,1,0:T(2,128)(2,1)}), bf16[64,2,3072]{2,1,0:T(2,128)(2,1)S(1)}, u32[]{:S(2)}, u32[]{:S(2)}) async-start(bf16[64,2,3072]{2,1,0:T(2,128)(2,1)} %reshape.312), calls=%async_computation.2 | async-start | bytes 1572864 | tf_op jit(solution)/shard_map/all_to_all | solution.py:79
  46.7 4.3 copy-start.11
  46.7 4.3 copy-start.13
  46.7 4.3 copy-start.15
  46.7 4.3 copy-start.17
  46.7 4.3 copy-start.19
  46.7 4.3 copy-start.21
  46.7 4.3 copy-start.23
  46.7 4.3 copy-start.25
  46.7 4.3 copy-start.27
  46.7 4.3 copy-start.29
  46.8 4.3 copy-start.31
  46.8 4.3 copy-start.33
  46.8 4.3 copy-start.35
  46.9 4.2 copy-start.50
  46.9 4.2 copy-start.52
  51.1 22.7 %copy-start.66 = (f32[192]{0:T(256)}, f32[192]{0:T(256)S(1)}, u32[]{:S(2)}) copy-start(f32[192]{0:T(256)S(1)} %broadcast_multiply_fusion.3) | copy-start | bytes 2308
  51.4 22.4 %copy-start.80 = (f32[192]{0:T(256)}, f32[192]{0:T(256)S(1)}, u32[]{:S(2)}) copy-start(f32[192]{0:T(256)S(1)} %multiply_reduce_fusion.17) | copy-start | bytes 2308
  52.0 21.9 %copy-start.89 = (s32[1,48]{1,0:T(1,128)S(1)}, s32[1,48]{1,0:T(1,128)}, u32[]{:S(2)}) copy-start(s32[1,48]{1,0:T(1,128)} %param.13) | copy-start | bytes 580
  283.8 5.4 copy-start.94
  299.3 4.4 copy-start.20
  299.3 4.4 copy-start.22
  299.3 4.3 copy-start.24
  299.4 4.3 copy-start.26
  299.4 4.3 copy-start.28
  299.4 4.3 copy-start.30
  299.4 4.3 copy-start.32
  299.4 4.3 copy-start.34
  299.4 4.3 copy-start.36
  299.4 9.0 %slice-start = ((s8[4718592]{0:T(1024)(128)(4,1)}), s8[4194304]{0:T(1024)(128)(4,1)S(1)}, s32[]{:S(2)}) async-start(s8[4718592]{0:T(1024)(128)(4,1)} %bitcast.25), calls=%async_computation.5 | async-start | bytes 8388608
  303.7 4.6 slice-start.1
  303.8 4.6 copy-start.83
  311.3 4.2 copy-start.44
  311.3 4.8 copy-start.43
  311.3 5.4 copy-start.42
  311.3 6.0 copy-start.41
  311.3 6.6 copy-start.40
  311.4 7.2 %copy-start.39 = (f32[1536]{0:T(1024)S(1)}, f32[1536]{0:T(1024)}, u32[]{:S(2)}) copy-start(f32[1536]{0:T(1024)} %get-tuple-element.15) | copy-start | bytes 18436
  311.4 7.8 %copy-start.90 = (s32[1,48]{1,0:T(1,128)S(1)}, s32[1,48]{1,0:T(1,128)}, u32[]{:S(2)}) copy-start(s32[1,48]{1,0:T(1,128)} %param.13) | copy-start | bytes 580
  325.7 10.2 %copy-start.38 = (f32[1536]{0:T(1024)S(1)}, f32[1536]{0:T(1024)}, u32[]{:S(2)}) copy-start(f32[1536]{0:T(1024)} %get-tuple-element.20) | copy-start | bytes 18436
  325.7 10.2 %copy-start.37 = (f32[1536]{0:T(1024)S(1)}, f32[1536]{0:T(1024)}, u32[]{:S(2)}) copy-start(f32[1536]{0:T(1024)} %get-tuple-element.22) | copy-start | bytes 18436
  325.7 154.5 %copy-start = (f32[192,1536]{1,0:T(8,128)S(1)}, f32[192,1536]{1,0:T(8,128)}, u32[]{:S(2)}) copy-start(f32[192,1536]{1,0:T(8,128)} %get-tuple-element.50) | copy-start | bytes 3538948
  325.7 318.9 %all-to-all-start.1 = ((bf16[64,2,3072]{2,1,0:T(2,128)(2,1)}), bf16[64,2,3072]{2,1,0:T(2,128)(2,1)}, u32[]{:S(2)}, u32[]{:S(2)}) async-start(bf16[64,2,3072]{2,1,0:T(2,128)(2,1)} %reshape.310), calls=%async_computation.1 | async-start | bytes 1572864 | tf_op jit(solution)/shard_map/all_to_all | solution.py:56
  333.0 310.1 %all-reduce.34.cloned.1.call-start = ((), (), s32[]{:S(2)}) async-start(), calls=%async_computation.4 | async-start | bytes 196608 | tf_op jit(solution)/shard_map/psum | solution.py:135
  480.2 5.1 copy-start.1
  480.2 5.1 copy-start.2
  480.2 5.1 copy-start.3
  480.2 5.1 copy-start.4
  480.2 5.1 copy-start.5
  644.6 4.9 copy-start.85
  644.6 4.9 copy-start.87
  644.6 4.9 copy-start.92
  (38 other events, 100.4 us)
Sparse Core Ops, SparseCore 0:
  10.7 273.0 all-gather.1
  339.4 303.6 all-reduce.33
where the time goes:
time: 659 us; the launch traced here: 658 us
  waiting for transfers between devices  385 us (58%)
  blocking collectives  143 us (22%)
  other arithmetic  43.2 us (7%)
  local copies, waits for them, and re-layouts  34.2 us (5%)
  starting transfers between devices  28.1 us (4%)
  between operations  15.3 us (2%)
  matrix products  9.28 us (1%)
    all_gather x1, waiting for transfers between devices, body(): gathered = lax.all_gather(bucket, 'dp', axis=0, tiled=True)  207 us
    psum x1, waiting for transfers between devices, body(): kernel_total, gain_total = lax.psum((kernel_term, gain_term), ('rep', 'dp'))  155 us
    psum x1, blocking collectives, body(): kernel_total, gain_total = lax.psum((kernel_term, gain_term), ('rep', 'dp'))  143 us
    all_to_all x1, waiting for transfers between devices, to_sources(): lax.all_to_all(outgoing, 'dp', split_axis=0, concat_axis=0, tiled=True)  19.9 us
  transfers between devices with their start and end apart: 5, of which 4 were waited for; matrix products, arithmetic and copies ran while one was open for 5% of the time, Pallas kernels for 0%

commit v1 on v0

--- a/solution.py
+++ b/solution.py
@@ -101,7 +101,8 @@
     updated = adam_step(master, moment, second, gradient)
     bucket = updated.astype(jnp.bfloat16)
     bucket_rows = bucket.shape[0]
-    gathered = lax.all_gather(bucket, "dp", axis=0, tiled=True)
+    sent = jnp.stack([bucket] * lax.axis_size("dp"))
+    gathered = jnp.concatenate(lax.all_to_all(sent, "dp", 0, 0), axis=0)
     weight = jnp.take(gathered.reshape(owners, bucket_rows, columns), bucket_order, axis=0).reshape(
         owners * bucket_rows, columns
     )

time: 659 us -> 514 us (0.78)
  waiting for transfers between devices: 385 us -> 269 us
  blocking collectives: 143 us -> 109 us
    all_gather x1 -> x0, waiting for transfers between devices: 207 us -> none  [body(): gathered = lax.all_gather(bucket, 'dp', axis=0, tiled=True)]
    all_to_all x0 -> x1, waiting for transfers between devices: none -> 87.5 us  [body(): gathered = jnp.concatenate(lax.all_to_all(sent, 'dp', 0, 0), axis=0)]
    psum x1, blocking collectives: 143 us -> 109 us  [body(): kernel_total, gain_total = lax.psum((kernel_term, gain_term), ('rep', 'dp'))]
    all_to_all x0 -> x1, starting transfers between devices: none -> 6.7 us  [body(): gathered = jnp.concatenate(lax.all_to_all(sent, 'dp', 0, 0), axis=0)]
where the time goes in v1:
time: 514 us; the launch traced here: 513 us
  waiting for transfers between devices  269 us (52%)
  blocking collectives  109 us (21%)
  other arithmetic  39.4 us (8%)
  local copies, waits for them, and re-layouts  36.8 us (7%)
  starting transfers between devices  33.8 us (7%)
  between operations  15.4 us (3%)
  matrix products  9.28 us (2%)
    psum x1, waiting for transfers between devices, body(): kernel_total, gain_total = lax.psum((kernel_term, gain_term), ('rep', 'dp'))  153 us
    psum x1, blocking collectives, body(): kernel_total, gain_total = lax.psum((kernel_term, gain_term), ('rep', 'dp'))  109 us
    all_to_all x1, waiting for transfers between devices, body(): gathered = jnp.concatenate(lax.all_to_all(sent, 'dp', 0, 0), axis=0)  87.5 us
    all_to_all x1, waiting for transfers between devices, to_sources(): lax.all_to_all(outgoing, 'dp', split_axis=0, concat_axis=0, tiled=True)  20.4 us
    all_to_all x1, starting transfers between devices, to_owners(): lax.all_to_all(has_block, 'dp', split_axis=0, concat_axis=0, tiled=True)  12.9 us
    unnamed x206, local copies, waits for them, and re-layouts  12.9 us
  transfers between devices with their start and end apart: 5, of which 4 were waited for; matrix products, arithmetic and copies ran while one was open for 5% of the time, Pallas kernels for 0%

profile of v1, /device:TPU:1, one launch (start us, length us, event | category | flops | bytes accessed | tf_op | source)
XLA Modules:
  0.0 513.3 jit_solution(4941417353320936954)
XLA Ops:
  7.2 0.7 fusion.15
  7.9 0.7 copy.26
  8.6 12.9 %all-to-all-start = ((bf16[64,1,1]{2,1,0:T(2,128)(2,1)}), bf16[64,1,1]{2,1,0:T(2,128)(2,1)S(1)}, u32[]{:S(2)}, u32[]{:S(2)}) async-start(bf16[64,1,1]{2,1,0:T(2,128)(2,1)} %copy.26), calls=%async_computation | async-start | bytes 65536 | tf_op jit(solution)/shard_map/all_to_all | solution.py:57
  21.6 1.3 reshape.264
  22.9 7.9 %all-to-all-done = bf16[64,1,1]{2,1,0:T(2,128)(2,1)S(1)} async-done(((bf16[64,1,1]{2,1,0:T(2,128)(2,1)}), bf16[64,1,1]{2,1,0:T(2,128)(2,1)S(1)}, u32[]{:S(2)}, u32[]{:S(2)}) %all-to-all-start) | async-done | bytes 160 | tf_op jit(solution)/shard_map/all_to_all | solution.py:57
  31.1 1.2 compare_reduce_fusion
  32.3 0.6 copy-done.88
  32.9 0.5 fusion
  33.4 0.5 broadcast.219
  33.9 1.1 reduce.36
  35.1 1.4 reshape.310
  36.5 4.6 all-to-all-start.3
  41.2 0.8 fusion.27
  42.0 20.4 %all-to-all-done.3 = bf16[64,2,3072]{2,1,0:T(2,128)(2,1)S(1)} async-done(((bf16[64,2,3072]{2,1,0:T(2,128)(2,1)}), bf16[64,2,3072]{2,1,0:T(2,128)(2,1)S(1)}, u32[]{:S(2)}, u32[]{:S(2)}) %all-to-all-start.3) | async-done | bytes 786464 | tf_op jit(solution)/shard_map/all_to_all | solution.py:79
  62.4 2.4 stack.2
  64.8 6.7 %all-to-all-start.1 = ((bf16[64,24,1536]{2,1,0:T(8,128)(2,1)}), bf16[64,24,1536]{2,1,0:T(8,128)(2,1)}, u32[]{:S(2)}, u32[]{:S(2)}) async-start(bf16[64,24,1536]{2,1,0:T(8,128)(2,1)} %stack.2), calls=%async_computation.1 | async-start | bytes 9437184 | tf_op jit(solution)/shard_map/all_to_all | solution.py:105
  71.8 0.6 slice.180
  72.4 0.7 broadcast_in_dim.23
  73.3 0.6 pad_clamp_fusion
  74.4 0.7 compare_convert_fusion.13
  75.3 3.9 fusion.26
  79.8 0.6 fusion.24
  80.3 2.0 reshape.311
  82.3 2.1 convolution_convert_fusion.2
  84.4 0.4 reshape.265
  84.8 87.5 %all-to-all-done.1 = bf16[64,24,1536]{2,1,0:T(8,128)(2,1)} async-done(((bf16[64,24,1536]{2,1,0:T(8,128)(2,1)}), bf16[64,24,1536]{2,1,0:T(8,128)(2,1)}, u32[]{:S(2)}, u32[]{:S(2)}) %all-to-all-start.1) | async-done | bytes 4718624 | tf_op jit(solution)/shard_map/all_to_all | solution.py:105
  172.3 5.4 %gather_fusion = bf16[64,24,1536]{2,1,0:T(8,128)(2,1)} fusion(bf16[64,24,1536]{2,1,0:T(8,128)(2,1)} %all-to-all-done.1, s32[1024]{0:T(1024)} %pad_clamp_fusion), kind=kCustom, calls=%fused_computation | custom fusion | bytes 9437440 | tf_op jit(solution)/shard_map/jit(_take)/gather | solution.py:106
  177.8 2.9 broadcast_select_fusion
  180.7 2.6 multiply_reduce_fusion
  183.4 0.3 multiply_reduce_fusion.18
  183.7 0.3 copy-done.51
  184.2 3.6 multiply_reduce_fusion.15
  187.9 4.3 multiply_reduce_fusion.5
  192.3 4.6 multiply_multiply_fusion.13
  196.9 0.9 bitcast_select_fusion
  197.8 2.0 convolution_convert_fusion.5
  199.9 2.3 reshape.262
  202.2 0.6 reshape.266
  202.9 0.6 reshape.267
  203.4 0.6 reshape.268
  204.0 0.6 reshape.269
  204.6 0.6 reshape.270
  205.2 0.6 reshape.271
  205.8 0.6 reshape.272
  206.4 0.6 reshape.274
  207.0 0.6 reshape.275
  207.6 1.5 fusion.1
  209.2 1.8 reduce.35
  211.0 3.2 reshape.308
  214.2 9.5 %all-to-all-start.2 = ((bf16[64,2,3072]{2,1,0:T(2,128)(2,1)}), bf16[64,2,3072]{2,1,0:T(2,128)(2,1)}, u32[]{:S(2)}, u32[]{:S(2)}) async-start(bf16[64,2,3072]{2,1,0:T(2,128)(2,1)} %reshape.308), calls=%async_computation.2 | async-start | bytes 1572864 | tf_op jit(solution)/shard_map/all_to_all | solution.py:56
  223.8 0.7 reshape.276
  224.5 0.7 reshape.277
  225.2 0.7 reshape.278
  225.9 0.7 reshape.279
  226.6 1.6 pad_add_fusion.6
  228.2 109.4 %psum.15 = f32[1536]{0:T(1024)S(1)} all-reduce(f32[1536]{0:T(1024)} %get-tuple-element.5), channel_id=1, replica_groups=mesh['rep'=8,'dp'=64] {'rep','dp'}, use_global_device_ids=true, to_apply=%region_26.27 | all-reduce | flops 1536 | bytes 12288 | tf_op jit(solution)/shard_map/psum | solution.py:136
  337.7 5.0 pad_add_fusion
  342.8 1.7 fusion.5
  344.5 0.6 broadcast_multiply_fusion.2
  345.1 153.3 %all-reduce.34.cloned.1.call-done = f32[15,1536]{1,0:T(8,128)} async-done(((f32[15,1536]{1,0:T(8,128)}), f32[15,1536]{1,0:T(8,128)}) %all-reduce.34.cloned.1.call-update) | async-done | bytes 92176 | tf_op jit(solution)/shard_map/psum | solution.py:136
  498.4 1.5 broadcast_multiply_fusion.1
  499.9 4.9 reshape.309
  504.9 0.6 convolution_convert_fusion.3
  505.5 1.0 reshape.263
  (222 shorter events, 1.8 us)
Async XLA Ops:
  8.6 22.2 %all-to-all-start = ((bf16[64,1,1]{2,1,0:T(2,128)(2,1)}), bf16[64,1,1]{2,1,0:T(2,128)(2,1)S(1)}, u32[]{:S(2)}, u32[]{:S(2)}) async-start(bf16[64,1,1]{2,1,0:T(2,128)(2,1)} %copy.26), calls=%async_computation | async-start | bytes 65536 | tf_op jit(solution)/shard_map/all_to_all | solution.py:57
  21.6 11.8 %copy-start.93 = (f32[32]{0:T(128)}, f32[32]{0:T(128)S(1)}, u32[]{:S(2)}) copy-start(f32[32]{0:T(128)S(1)} %iota_convert_fusion) | copy-start | bytes 388
  35.0 6.2 %copy-start.8 = (f32[24,1536]{1,0:T(8,128)S(1)}, f32[24,1536]{1,0:T(8,128)}, u32[]{:S(2)}) copy-start(f32[24,1536]{1,0:T(8,128)} %param.16) | copy-start | bytes 442372
  35.0 6.1 %copy-start.9 = (f32[24,1536]{1,0:T(8,128)S(1)}, f32[24,1536]{1,0:T(8,128)}, u32[]{:S(2)}) copy-start(f32[24,1536]{1,0:T(8,128)} %param.19) | copy-start | bytes 442372
  35.0 6.1 %copy-start.10 = (f32[24,1536]{1,0:T(8,128)S(1)}, f32[24,1536]{1,0:T(8,128)}, u32[]{:S(2)}) copy-start(f32[24,1536]{1,0:T(8,128)} %param.18) | copy-start | bytes 442372
  35.0 6.1 %copy-start.11 = (f32[24,1536]{1,0:T(8,128)S(1)}, f32[24,1536]{1,0:T(8,128)}, u32[]{:S(2)}) copy-start(f32[24,1536]{1,0:T(8,128)} %param.17) | copy-start | bytes 442372
  36.5 25.9 %all-to-all-start.3 = ((bf16[64,2,3072]{2,1,0:T(2,128)(2,1)}), bf16[64,2,3072]{2,1,0:T(2,128)(2,1)S(1)}, u32[]{:S(2)}, u32[]{:S(2)}) async-start(bf16[64,2,3072]{2,1,0:T(2,128)(2,1)} %reshape.310), calls=%async_computation.3 | async-start | bytes 1572864 | tf_op jit(solution)/shard_map/all_to_all | solution.py:79
  64.8 6.7 %copy-start.97 = (s32[1,8]{1,0:T(1,128)S(1)}, s32[1,8]{1,0:T(1,128)}, u32[]{:S(2)}) copy-start(s32[1,8]{1,0:T(1,128)} %param.12) | copy-start | bytes 100
  64.8 7.5 %copy-start.98 = (s32[64]{0:T(128)S(1)}, s32[64]{0:T(128)}, u32[]{:S(2)}) copy-start(s32[64]{0:T(128)} %param.20) | copy-start | bytes 772
  64.8 8.3 %copy-start.6 = (bf16[192,1536]{1,0:T(8,128)(2,1)S(1)}, bf16[192,1536]{1,0:T(8,128)(2,1)}, u32[]{:S(2)}) copy-start(bf16[192,1536]{1,0:T(8,128)(2,1)} %param.11) | copy-start | bytes 1769476
  64.8 107.5 %all-to-all-start.1 = ((bf16[64,24,1536]{2,1,0:T(8,128)(2,1)}), bf16[64,24,1536]{2,1,0:T(8,128)(2,1)}, u32[]{:S(2)}, u32[]{:S(2)}) async-start(bf16[64,24,1536]{2,1,0:T(8,128)(2,1)} %stack.2), calls=%async_computation.1 | async-start | bytes 9437184 | tf_op jit(solution)/shard_map/all_to_all | solution.py:105
  74.2 5.0 copy-start.13
  74.2 5.0 copy-start.15
  74.2 5.0 copy-start.17
  74.3 5.0 copy-start.19
  74.3 5.0 copy-start.21
  74.3 5.0 copy-start.23
  74.3 5.0 copy-start.25
  74.3 5.0 copy-start.27
  74.3 5.0 copy-start.29
  74.3 5.0 copy-start.31
  74.3 5.0 copy-start.33
  74.3 5.0 copy-start.35
  74.3 5.0 copy-start.37
  75.1 4.2 copy-start.50
  75.1 4.2 copy-start.70
  75.1 4.3 copy-start.72
  75.1 4.3 copy-start.74
  75.1 4.3 copy-start.76
  75.1 4.3 copy-start.80
  75.2 4.2 copy-start.52
  84.8 93.0 %copy-start.96 = (pred[64]{0:T(512)(128)(4,1)S(1)}, pred[64]{0:T(512)(128)(4,1)}, u32[]{:S(2)}) copy-start(pred[64]{0:T(512)(128)(4,1)} %copy-done.95) | copy-start | bytes 196
  187.8 4.4 copy-start.22
  187.9 4.4 copy-start.24
  187.9 4.3 copy-start.26
  187.9 4.3 copy-start.28
  187.9 4.3 copy-start.30
  187.9 4.3 copy-start.32
  187.9 4.3 copy-start.34
  187.9 4.3 copy-start.36
  187.9 4.3 copy-start.38
  187.9 9.0 %slice-start = ((s8[4718592]{0:T(1024)(128)(4,1)}), s8[4194304]{0:T(1024)(128)(4,1)S(1)}, s32[]{:S(2)}) async-start(s8[4718592]{0:T(1024)(128)(4,1)} %bitcast.24), calls=%async_computation.5 | async-start | bytes 8388608
  192.3 4.6 slice-start.1
  192.3 4.6 copy-start.85
  199.8 4.2 copy-start.46
  199.8 4.8 copy-start.45
  199.8 5.4 %copy-start.44 = (f32[1536]{0:T(1024)S(1)}, f32[1536]{0:T(1024)}, u32[]{:S(2)}) copy-start(f32[1536]{0:T(1024)} %get-tuple-element.12) | copy-start | bytes 18436
  199.9 6.0 %copy-start.43 = (f32[1536]{0:T(1024)S(1)}, f32[1536]{0:T(1024)}, u32[]{:S(2)}) copy-start(f32[1536]{0:T(1024)} %get-tuple-element.13) | copy-start | bytes 18436
  199.9 6.6 %copy-start.42 = (f32[1536]{0:T(1024)S(1)}, f32[1536]{0:T(1024)}, u32[]{:S(2)}) copy-start(f32[1536]{0:T(1024)} %get-tuple-element.14) | copy-start | bytes 18436
  199.9 7.2 %copy-start.41 = (f32[1536]{0:T(1024)S(1)}, f32[1536]{0:T(1024)}, u32[]{:S(2)}) copy-start(f32[1536]{0:T(1024)} %get-tuple-element.15) | copy-start | bytes 18436
  199.9 7.8 %copy-start.92 = (s32[1,48]{1,0:T(1,128)S(1)}, s32[1,48]{1,0:T(1,128)}, u32[]{:S(2)}) copy-start(s32[1,48]{1,0:T(1,128)} %param.13) | copy-start | bytes 580
  214.2 12.3 %copy-start.40 = (f32[1536]{0:T(1024)S(1)}, f32[1536]{0:T(1024)}, u32[]{:S(2)}) copy-start(f32[1536]{0:T(1024)} %get-tuple-element.20) | copy-start | bytes 18436
  214.2 12.3 %copy-start.39 = (f32[1536]{0:T(1024)S(1)}, f32[1536]{0:T(1024)}, u32[]{:S(2)}) copy-start(f32[1536]{0:T(1024)} %get-tuple-element.22) | copy-start | bytes 18436
  214.2 123.4 %copy-start = (f32[192,1536]{1,0:T(8,128)S(1)}, f32[192,1536]{1,0:T(8,128)}, u32[]{:S(2)}) copy-start(f32[192,1536]{1,0:T(8,128)} %get-tuple-element.50) | copy-start | bytes 3538948
  214.2 285.7 %all-to-all-start.2 = ((bf16[64,2,3072]{2,1,0:T(2,128)(2,1)}), bf16[64,2,3072]{2,1,0:T(2,128)(2,1)}, u32[]{:S(2)}, u32[]{:S(2)}) async-start(bf16[64,2,3072]{2,1,0:T(2,128)(2,1)} %reshape.308), calls=%async_computation.2 | async-start | bytes 1572864 | tf_op jit(solution)/shard_map/all_to_all | solution.py:56
  223.7 274.7 %all-reduce.34.cloned.1.call-start = ((), (), s32[]{:S(2)}) async-start(), calls=%async_computation.4 | async-start | bytes 196608 | tf_op jit(solution)/shard_map/psum | solution.py:136
  337.6 5.1 copy-start.1
  337.6 5.1 copy-start.2
  337.6 5.1 copy-start.3
  337.6 5.1 copy-start.4
  337.7 5.1 copy-start.5
  499.9 4.9 copy-start.87
  499.9 4.9 copy-start.89
  499.9 4.9 copy-start.94
  (42 other events, 110.6 us)
Sparse Core Ops, SparseCore 0:
  230.1 268.2 all-reduce.33
